TPU v7x, 256 devices: a whole 4x4x8 slice. The times are simulated.
256 devices in a mesh: seq: 64 (over y, z, core), head: 4 (over x).
Axes of the slice: x: 4, y: 4, z: 8, core: 2. Of those that a mesh axis runs over, the one named last changes fastest.
Arguments:
- tokens: bfloat16 [16384, 2048], P('seq')
- w_qkv: bfloat16 [2048, 3, 2048], P(None, None, 'head'), may hold values from -0.125 to 0.125
- w_out: bfloat16 [2048, 2048], P('head'), may hold values from -0.125 to 0.125
- norm_gain: float32 [2048], replicated, may hold values from 0.25 to 1.75
- w_label: bfloat16 [2048, 128], replicated, may hold values from -0.125 to 0.125
- offset_mid: int32 [16], P('head'), may hold values from 0 to 7
- offset_far: int32 [16], P('head'), may hold values from 0 to 63
Outputs:
- logits: float32 [16384, 128], P('seq')
All inputs are finite; a program needn't handle non-finite values.
Results may differ from a plain program's by a relative error of at most 0.023.
The roundings to bfloat16 on the way count: a program that leaves them out, or rounds other values in their place, can miss the bound.
Values may be sent and summed in bfloat16 or wider, within the bound.
No kernel may reach another device: no remote copies, remote signals or barrier semaphores. Data moves between devices by JAX's collectives and lax.ppermute only.
A program may use at most 64 MiB of HBM per device.

v0:
```python
import jax
import jax.numpy as jnp
from jax import lax
from jax.sharding import PartitionSpec as P

SPAN = 8


def from_behind(block, axis, distance):
    devices = range(lax.axis_size(axis))
    route = [((i - distance) % len(devices), i) for i in devices]
    return lax.ppermute(block, axis, route)


def attend(queries, keys, values):
    scores = jnp.einsum(
        "rhe,she->hrs", queries, keys, preferred_element_type=jnp.float32
    ) / jnp.sqrt(jnp.float32(queries.shape[2]))
    top = jnp.max(scores, axis=-1)
    weights = jnp.exp(scores - top[..., None])
    total = jnp.sum(weights, axis=-1)
    summed = jnp.einsum(
        "hrs,she->rhe", weights.astype(jnp.bfloat16), values, preferred_element_type=jnp.float32
    )
    return (top.T, total.T, summed)


def select_rows(array, offsets, rate):
    rows = array.shape[0] // rate
    shaped = array.reshape(rows, rate, array.shape[1], array.shape[2])
    index = jnp.broadcast_to(
        offsets[None, None, :, None], (rows, 1, array.shape[1], array.shape[2])
    )
    return jnp.take_along_axis(shaped, index, axis=1)[:, 0]


def spread_rows(parts, offsets, rate):
    top, total, summed = parts
    rows = top.shape[0]
    marks = jnp.arange(rate, dtype=jnp.int32)[None, :, None] == offsets[None, None, :]
    top_full = jnp.where(marks, top[:, None, :], jnp.float32(-1e30)).reshape(rows * rate, -1)
    total_full = jnp.where(marks, total[:, None, :], jnp.float32(0.0)).reshape(rows * rate, -1)
    sum_full = jnp.where(marks[..., None], summed[:, None], jnp.float32(0.0)).reshape(
        rows * rate, summed.shape[1], summed.shape[2]
    )
    return (top_full, total_full, sum_full)


def body(tokens, w_qkv, w_out, norm_gain, w_label, offset_mid, offset_far):
    tok_rows = tokens.shape[0]
    local_heads = offset_mid.shape[0]
    head_size = w_qkv.shape[2] // local_heads
    qkv = jnp.einsum("td,dce->tce", tokens, w_qkv, preferred_element_type=jnp.float32).astype(
        jnp.bfloat16
    )
    qkv = qkv.reshape(tok_rows, 3, local_heads, head_size)
    queries, keys, values = (qkv[:, 0], qkv[:, 1], qkv[:, 2])
    seq_count = lax.axis_size("seq")
    near = attend(queries, keys, values)
    mid_q = select_rows(queries, offset_mid, SPAN)
    mid_kv = jnp.stack(
        [select_rows(keys, offset_mid, SPAN), select_rows(values, offset_mid, SPAN)], axis=0
    )
    mid_rows = mid_kv.shape[1]
    position = (lax.axis_index("seq") + SPAN // 2) % SPAN
    lower_pieces = []
    upper_pieces = []
    for step_back in range(1, SPAN):
        lower_pieces.insert(0, from_behind(mid_kv, "seq", step_back))
        upper_pieces.append(from_behind(mid_kv, "seq", -step_back))
    window = jnp.concatenate(lower_pieces + [mid_kv] + upper_pieces, axis=1)
    gathered = lax.dynamic_slice_in_dim(
        window, (SPAN - 1 - position) * mid_rows, SPAN * mid_rows, 1
    )
    middle = spread_rows(attend(mid_q, gathered[0], gathered[1]), offset_mid, SPAN)
    far_q = select_rows(queries, offset_far, seq_count)
    far_kv = jnp.stack(
        [select_rows(keys, offset_far, seq_count), select_rows(values, offset_far, seq_count)],
        axis=0,
    )
    far_all = lax.all_gather(far_kv, "seq", axis=1, tiled=True)
    distant = spread_rows(attend(far_q, far_all[0], far_all[1]), offset_far, seq_count)
    branches = [near, middle, distant]
    peak = jnp.maximum(jnp.maximum(near[0], middle[0]), distant[0])
    upper = jnp.zeros((tok_rows, local_heads, head_size), jnp.float32)
    lower = jnp.zeros((tok_rows, local_heads), jnp.float32)
    for top, total, summed in branches:
        factor = jnp.exp(top - peak)
        upper = upper + factor[..., None] * summed
        lower = lower + factor * total
    attn = (
        (upper / lower[..., None]).astype(jnp.bfloat16).reshape(tok_rows, local_heads * head_size)
    )
    partial_out = jnp.dot(attn, w_out, preferred_element_type=jnp.float32)
    projected = lax.psum(partial_out.astype(jnp.bfloat16), "head").astype(jnp.float32)
    mixed = tokens.astype(jnp.float32) + projected
    mean_sq = jnp.mean(mixed * mixed, axis=-1)
    scaled = (mixed * norm_gain).astype(jnp.bfloat16)
    product = jnp.dot(scaled, w_label, preferred_element_type=jnp.float32)
    return product / jnp.sqrt(mean_sq + 1e-05)[:, None]


def solution(mesh):
    return jax.shard_map(
        body,
        mesh=mesh,
        in_specs=(
            P("seq", None),
            P(None, None, "head"),
            P("head", None),
            P(),
            P(),
            P("head"),
            P("head"),
        ),
        out_specs=P("seq", None),
        check_vma=False,
    )
```

profile of v0, /device:TPU:8, one launch (start us, length us, event | category | flops | bytes accessed | tf_op | source)
XLA Modules:
  0.0 969.6 jit_solution(3699433661671569265)
XLA Ops:
  6.5 5.9 convolution_convert_fusion.1
  12.5 1.7 reshape.163
  14.2 1.0 fusion.55
  16.3 235.5 %gather_fusion.1 = bf16[16384]{0:T(1024)(128)(2,1)} fusion(bf16[32,8,4,128]{3,1,0,2:T(8,128)(2,1)S(1)} %get-tuple-element.34, s32[16384]{0:T(1024)S(1)} %bitcast.149), kind=kCustom, calls=%fused_computation.2.clone | custom fusion | bytes 327680 | tf_op jit(solution)/shard_map/jit(take_along_axis)/gather | solution.py:34
  251.7 236.4 %gather_fusion.2 = bf16[16384]{0:T(1024)(128)(2,1)} fusion(bf16[32,8,4,128]{3,1,0,2:T(8,128)(2,1)S(1)} %get-tuple-element.20, s32[16384]{0:T(1024)S(1)} %bitcast.150), kind=kCustom, calls=%fused_computation.3.clone | custom fusion | bytes 327680 | tf_op jit(solution)/shard_map/jit(take_along_axis)/gather | solution.py:34
  488.1 0.9 fusion.28
  489.6 4.1 collective-permute-start
  493.6 4.0 collective-permute-start.1
  498.0 3.2 collective-permute-start.3
  501.2 2.6 collective-permute-start.4
  503.8 2.2 fusion.59
  507.2 0.9 copy.77
  508.1 236.0 %gather_fusion = bf16[16384]{0:T(1024)(128)(2,1)} fusion(bf16[32,8,4,128]{3,1,0,2:T(8,128)(2,1)S(1)} %bitcast.152, s32[16384]{0:T(1024)S(1)} %bitcast.151), kind=kCustom, calls=%fused_computation.clone | custom fusion | bytes 327680 | tf_op jit(solution)/shard_map/jit(take_along_axis)/gather | solution.py:34
  744.2 22.2 %gather_fusion.5 = bf16[2048]{0:T(1024)(128)(2,1)S(1)} fusion(bf16[4,64,4,128]{3,1,0,2:T(8,128)(2,1)S(1)} %bitcast.158, s32[2048]{0:T(1024)S(1)} %bitcast.154), kind=kCustom, calls=%fused_computation.5.clone | custom fusion | bytes 40960 | tf_op jit(solution)/shard_map/jit(take_along_axis)/gather | solution.py:34
  766.4 22.2 %gather_fusion.4 = bf16[2048]{0:T(1024)(128)(2,1)S(1)} fusion(bf16[4,64,4,128]{3,1,0,2:T(8,128)(2,1)S(1)} %bitcast.157, s32[2048]{0:T(1024)S(1)} %bitcast.155), kind=kCustom, calls=%fused_computation.4.clone | custom fusion | bytes 40960 | tf_op jit(solution)/shard_map/jit(take_along_axis)/gather | solution.py:34
  788.6 22.2 %gather_fusion.3 = bf16[2048]{0:T(1024)(128)(2,1)S(1)} fusion(bf16[4,64,4,128]{3,1,0,2:T(8,128)(2,1)S(1)} %bitcast.153, s32[2048]{0:T(1024)S(1)} %bitcast.156), kind=kCustom, calls=%fused_computation.1.clone | custom fusion | bytes 40960 | tf_op jit(solution)/shard_map/jit(take_along_axis)/gather | solution.py:34
  810.8 48.7 %all_gather.3 = bf16[2,256,4,128]{3,2,0,1:T(4,128)(2,1)S(1)} all-gather(bf16[2,4,4,128]{3,2,0,1:T(4,128)(2,1)S(1)} %copy.67), channel_id=1, replica_groups=mesh['seq'=64,'head'=4] {'seq'}, dimensions={1}, use_global_device_ids=true | all-gather | bytes 532480 | tf_op jit(solution)/shard_map/all_gather | solution.py:81
  860.9 0.6 broadcast_in_dim.167
  861.5 0.7 broadcast_in_dim.168
  862.2 0.7 broadcast_in_dim.173
  862.9 0.7 broadcast_in_dim.174
  863.5 0.8 broadcast_in_dim.183
  864.4 2.0 copy.73
  866.4 1.3 collective-permute-start.5
  867.7 0.8 constant_dynamic-update-slice_fusion.14
  868.6 0.9 constant_dynamic-update-slice_fusion.13
  869.5 3.9 collective-permute-start.7
  873.4 0.9 constant_dynamic-update-slice_fusion.12
  874.2 0.8 collective-permute-start.8
  875.1 0.9 constant_dynamic-update-slice_fusion.11
  876.0 0.9 constant_dynamic-update-slice_fusion.10
  876.9 1.3 collective-permute-start.10
  878.2 1.7 collective-permute-start.11
  879.9 5.6 collective-permute-start.12
  885.5 0.8 collective-permute-start.13
  886.8 1.1 collective-permute-done.11
  887.9 6.6 collective-permute-done.12
  894.6 0.9 copy-done.5
  895.6 1.1 fusion.58
  897.2 1.2 convolution_bitcast_fusion.1
  898.4 0.9 broadcast_bitcast_fusion
  899.2 2.0 copy.71
  901.3 0.7 fusion.43
  902.0 1.6 fusion.4
  903.6 1.7 convolution_convert_fusion
  905.4 52.9 %all-reduce.2.cloned.1.call-done = bf16[256,2048]{1,0:T(8,128)(2,1)} async-done(((bf16[256,2048]{1,0:T(8,128)(2,1)}), bf16[256,2048]{1,0:T(8,128)(2,1)}) %all-reduce.2.cloned.1.call-update) | async-done | bytes 1048592 | tf_op jit(solution)/shard_map/psum | solution.py:95
  958.2 2.0 multiply_reduce_fusion
  960.2 2.5 convolution_divide_fusion
  (89 shorter events, 6.2 us)
Async XLA Ops:
  6.5 897.1 %copy-start = (bf16[512,2048]{1,0:T(8,128)(2,1)S(1)}, bf16[512,2048]{1,0:T(8,128)(2,1)}, u32[]{:S(2)}) copy-start(bf16[512,2048]{1,0:T(8,128)(2,1)} %param.13) | copy-start | bytes 6291460
  6.5 8.7 copy-start.6
  6.5 8.7 copy-start.9
  6.5 951.7 %all-reduce.2.cloned.1.call-start = ((), (), s32[]{:S(2)}) async-start(), calls=%async_computation | async-start | bytes 2097152 | tf_op jit(solution)/shard_map/psum | solution.py:95
  15.2 0.8 copy-start.3
  15.2 472.9 %copy-start.8 = (s32[4]{0:T(128)}, s32[4]{0:T(128)S(1)}, u32[]{:S(2)}) copy-start(s32[4]{0:T(128)S(1)} %broadcast_add_fusion.1) | copy-start | bytes 52
  15.8 472.3 %copy-start.7 = (pred[4]{0:T(512)(128)(4,1)}, pred[4]{0:T(512)(128)(4,1)S(1)}, u32[]{:S(2)}) copy-start(pred[4]{0:T(512)(128)(4,1)S(1)} %get-tuple-element.36) | copy-start | bytes 16
  251.7 252.0 %copy-start.2 = (bf16[256,1,4,128]{3,2,0,1:T(4,128)(2,1)S(1)}, bf16[256,1,4,128]{3,2,0,1:T(4,128)(2,1)}, u32[]{:S(2)}) copy-start(bf16[256,1,4,128]{3,2,0,1:T(4,128)(2,1)} %get-tuple-element.12) | copy-start | bytes 786436
  489.6 376.8 %collective-permute-start = (bf16[2,32,4,128]{3,1,2,0:T(8,128)(2,1)}, bf16[2,32,4,128]{3,1,2,0:T(8,128)(2,1)}, u32[]{:S(2)}, u32[]{:S(2)}) collective-permute-start(bf16[2,32,4,128]{3,1,2,0:T(8,128)(2,1)} %pad_maximum_fusion), channel_id=1, source_target_pairs={{228,0},{232,4},{236,8},{240,12},{244,16},{248,20},{252,24},{0,28}... | collective-permute-start | bytes 196616 | tf_op jit(solution)/shard_map/ppermute | solution.py:12
  493.6 374.9 %collective-permute-start.1 = (bf16[2,32,4,128]{3,1,2,0:T(8,128)(2,1)}, bf16[2,32,4,128]{3,1,2,0:T(8,128)(2,1)}, u32[]{:S(2)}, u32[]{:S(2)}) collective-permute-start(bf16[2,32,4,128]{3,1,2,0:T(8,128)(2,1)} %pad_maximum_fusion), channel_id=1, source_target_pairs={{232,0},{236,4},{240,8},{244,12},{248,16},{252,20},{0,24},{4,28},{... | collective-permute-start | bytes 196616 | tf_op jit(solution)/shard_map/ppermute | solution.py:12
  497.7 371.8 %collective-permute-start.2 = (bf16[2,32,4,128]{3,1,2,0:T(8,128)(2,1)}, bf16[2,32,4,128]{3,1,2,0:T(8,128)(2,1)}, u32[]{:S(2)}, u32[]{:S(2)}) collective-permute-start(bf16[2,32,4,128]{3,1,2,0:T(8,128)(2,1)} %pad_maximum_fusion), channel_id=1, source_target_pairs={{236,0},{240,4},{244,8},{248,12},{252,16},{0,20},{4,24},{8,28},{12... | collective-permute-start | bytes 196616 | tf_op jit(solution)/shard_map/ppermute | solution.py:12
  498.0 376.3 %collective-permute-start.3 = (bf16[2,32,4,128]{3,1,2,0:T(8,128)(2,1)}, bf16[2,32,4,128]{3,1,2,0:T(8,128)(2,1)}, u32[]{:S(2)}, u32[]{:S(2)}) collective-permute-start(bf16[2,32,4,128]{3,1,2,0:T(8,128)(2,1)} %pad_maximum_fusion), channel_id=1, source_target_pairs={{240,0},{244,4},{248,8},{252,12},{0,16},{4,20},{8,24},{12,28},{16,... | collective-permute-start | bytes 196616 | tf_op jit(solution)/shard_map/ppermute | solution.py:12
  501.2 374.8 %collective-permute-start.4 = (bf16[2,32,4,128]{3,1,2,0:T(8,128)(2,1)}, bf16[2,32,4,128]{3,1,2,0:T(8,128)(2,1)}, u32[]{:S(2)}, u32[]{:S(2)}) collective-permute-start(bf16[2,32,4,128]{3,1,2,0:T(8,128)(2,1)} %pad_maximum_fusion), channel_id=1, source_target_pairs={{244,0},{248,4},{252,8},{0,12},{4,16},{8,20},{12,24},{16,28},{20,3... | collective-permute-start | bytes 196616 | tf_op jit(solution)/shard_map/ppermute | solution.py:12
  508.1 236.0 %copy-start.10 = (pred[4]{0:T(512)(128)(4,1)S(1)}, pred[4]{0:T(512)(128)(4,1)}, u32[]{:S(2)}) copy-start(pred[4]{0:T(512)(128)(4,1)} %get-tuple-element.35) | copy-start | bytes 16
  788.6 71.4 %copy-start.1 = (f32[4,256,256]{1,2,0:T(8,128)S(1)}, f32[4,256,256]{1,2,0:T(8,128)}, u32[]{:S(2)}) copy-start(f32[4,256,256]{1,2,0:T(8,128)} %get-tuple-element.32) | copy-start | bytes 3145732
  866.4 10.5 %collective-permute-start.5 = (bf16[2,32,4,128]{3,1,2,0:T(8,128)(2,1)}, bf16[2,32,4,128]{3,1,2,0:T(8,128)(2,1)S(1)}, u32[]{:S(2)}, u32[]{:S(2)}) collective-permute-start(bf16[2,32,4,128]{3,1,2,0:T(8,128)(2,1)} %pad_maximum_fusion), channel_id=1, source_target_pairs={{248,0},{252,4},{0,8},{4,12},{8,16},{12,20},{16,24},{20,28},{24,32... | collective-permute-start | bytes 196616 | tf_op jit(solution)/shard_map/ppermute | solution.py:12
  868.5 9.7 collective-permute-start.6
  869.5 10.4 %collective-permute-start.7 = (bf16[2,32,4,128]{3,1,2,0:T(8,128)(2,1)}, bf16[2,32,4,128]{3,1,2,0:T(8,128)(2,1)S(1)}, u32[]{:S(2)}, u32[]{:S(2)}) collective-permute-start(bf16[2,32,4,128]{3,1,2,0:T(8,128)(2,1)} %pad_maximum_fusion), channel_id=1, source_target_pairs={{4,0},{8,4},{12,8},{16,12},{20,16},{24,20},{28,24},{32,28},{36,32}... | collective-permute-start | bytes 196616 | tf_op jit(solution)/shard_map/ppermute | solution.py:12
  874.2 11.2 %collective-permute-start.8 = (bf16[2,32,4,128]{3,1,2,0:T(8,128)(2,1)}, bf16[2,32,4,128]{3,1,2,0:T(8,128)(2,1)S(1)}, u32[]{:S(2)}, u32[]{:S(2)}) collective-permute-start(bf16[2,32,4,128]{3,1,2,0:T(8,128)(2,1)} %pad_maximum_fusion), channel_id=1, source_target_pairs={{8,0},{12,4},{16,8},{20,12},{24,16},{28,20},{32,24},{36,28},{40,32... | collective-permute-start | bytes 196616 | tf_op jit(solution)/shard_map/ppermute | solution.py:12
  875.9 10.4 %collective-permute-start.9 = (bf16[2,32,4,128]{3,1,2,0:T(8,128)(2,1)}, bf16[2,32,4,128]{3,1,2,0:T(8,128)(2,1)S(1)}, u32[]{:S(2)}, u32[]{:S(2)}) collective-permute-start(bf16[2,32,4,128]{3,1,2,0:T(8,128)(2,1)} %pad_maximum_fusion), channel_id=1, source_target_pairs={{12,0},{16,4},{20,8},{24,12},{28,16},{32,20},{36,24},{40,28},{44,3... | collective-permute-start | bytes 196616 | tf_op jit(solution)/shard_map/ppermute | solution.py:12
  876.9 9.9 %collective-permute-start.10 = (bf16[2,32,4,128]{3,1,2,0:T(8,128)(2,1)}, bf16[2,32,4,128]{3,1,2,0:T(8,128)(2,1)S(1)}, u32[]{:S(2)}, u32[]{:S(2)}) collective-permute-start(bf16[2,32,4,128]{3,1,2,0:T(8,128)(2,1)} %pad_maximum_fusion), channel_id=1, source_target_pairs={{16,0},{20,4},{24,8},{28,12},{32,16},{36,20},{40,24},{44,28},{48,3... | collective-permute-start | bytes 196616 | tf_op jit(solution)/shard_map/ppermute | solution.py:12
  878.2 9.7 %collective-permute-start.11 = (bf16[2,32,4,128]{3,1,2,0:T(8,128)(2,1)}, bf16[2,32,4,128]{3,1,2,0:T(8,128)(2,1)S(1)}, u32[]{:S(2)}, u32[]{:S(2)}) collective-permute-start(bf16[2,32,4,128]{3,1,2,0:T(8,128)(2,1)} %pad_maximum_fusion), channel_id=1, source_target_pairs={{20,0},{24,4},{28,8},{32,12},{36,16},{40,20},{44,24},{48,28},{52,3... | collective-permute-start | bytes 196616 | tf_op jit(solution)/shard_map/ppermute | solution.py:12
  879.9 14.6 %collective-permute-start.12 = (bf16[2,32,4,128]{3,1,2,0:T(8,128)(2,1)}, bf16[2,32,4,128]{3,1,2,0:T(8,128)(2,1)S(1)}, u32[]{:S(2)}, u32[]{:S(2)}) collective-permute-start(bf16[2,32,4,128]{3,1,2,0:T(8,128)(2,1)} %pad_maximum_fusion), channel_id=1, source_target_pairs={{24,0},{28,4},{32,8},{36,12},{40,16},{44,20},{48,24},{52,28},{56,3... | collective-permute-start | bytes 196616 | tf_op jit(solution)/shard_map/ppermute | solution.py:12
  885.5 9.1 collective-permute-start.13
  894.6 1.0 copy-start.5
  897.1 63.1 %copy-start.11 = (f32[2048]{0:T(1024)S(1)}, f32[2048]{0:T(1024)}, u32[]{:S(2)}) copy-start(f32[2048]{0:T(1024)} %param.14) | copy-start | bytes 24580
  903.6 56.6 %copy-start.4 = (bf16[256,2048]{1,0:T(8,128)(2,1)S(1)}, bf16[256,2048]{1,0:T(8,128)(2,1)}, u32[]{:S(2)}) copy-start(bf16[256,2048]{1,0:T(8,128)(2,1)} %param.11) | copy-start | bytes 3145732
Sparse Core Ops, SparseCore 0:
  905.5 52.6 all-reduce.1
where the time goes:
time: 970 us
  local copies, waits for them, and re-layouts  793 us (82%)
  waiting for transfers between devices  61.1 us (6%)
  blocking collectives  48.7 us (5%)
  starting transfers between devices  29.6 us (3%)
  matrix products  16.8 us (2%)
  between operations  13.7 us (1%)
    gather x7, local copies, waits for them, and re-layouts, select_rows(): return jnp.take_along_axis(shaped, index, axis=1)[:, 0]  774 us
    psum x1, waiting for transfers between devices, body(): lax.psum(partial_out.astype(jnp.bfloat16), 'head').astype(jnp.float32)  52.9 us
    all_gather x1, blocking collectives, body(): far_all = lax.all_gather(far_kv, 'seq', axis=1, tiled=True)  48.7 us
    ppermute x14, starting transfers between devices, from_behind(): return lax.ppermute(block, axis, route)  29.6 us
  transfers between devices with their start and end apart: 15, of which 5 were waited for; matrix products, arithmetic and copies ran while one was open for 33% of the time, Pallas kernels for 0%

commit v1 on v0

--- a/solution.py
+++ b/solution.py
@@ -78,7 +78,9 @@
         [select_rows(keys, offset_far, seq_count), select_rows(values, offset_far, seq_count)],
         axis=0,
     )
-    far_all = lax.all_gather(far_kv, "seq", axis=1, tiled=True)
+    far_all = jnp.concatenate(
+        lax.all_to_all(jnp.stack([far_kv] * lax.axis_size("seq")), "seq", 0, 0), axis=1
+    )
     distant = spread_rows(attend(far_q, far_all[0], far_all[1]), offset_far, seq_count)
     branches = [near, middle, distant]
     peak = jnp.maximum(jnp.maximum(near[0], middle[0]), distant[0])

time: 970 us -> 787 us (0.81)
  local copies, waits for them, and re-layouts: 793 us -> 650 us
  blocking collectives: 48.7 us -> 0 us
  starting transfers between devices: 29.6 us -> 40.9 us
    gather x7, local copies, waits for them, and re-layouts: 774 us -> 630 us  [select_rows(): return jnp.take_along_axis(shaped, index, axis=1)[:, 0]]
    all_gather x1 -> x0, blocking collectives: 48.7 us -> none  [body(): far_all = lax.all_gather(far_kv, 'seq', axis=1, tiled=True)]
  transfers between devices with their start and end apart: 15 -> 16, of which waited for: 5 -> 3; matrix products, arithmetic and copies ran while one was open for 33% -> 41% of each run, Pallas kernels for 0% -> 0%
where the time goes in v1:
time: 787 us; the launch traced here: 786 us
  local copies, waits for them, and re-layouts  650 us (83%)
  waiting for transfers between devices  58.5 us (7%)
  starting transfers between devices  40.9 us (5%)
  matrix products  15.9 us (2%)
  between operations  13.9 us (2%)
    gather x7, local copies, waits for them, and re-layouts, select_rows(): return jnp.take_along_axis(shaped, index, axis=1)[:, 0]  630 us
    psum x1, waiting for transfers between devices, body(): lax.psum(partial_out.astype(jnp.bfloat16), 'head').astype(jnp.float32)  52.4 us
    ppermute x14, starting transfers between devices, from_behind(): return lax.ppermute(block, axis, route)  33.1 us
  transfers between devices with their start and end apart: 16, of which 3 were waited for; matrix products, arithmetic and copies ran while one was open for 41% of the time, Pallas kernels for 0%

profile of v1, /device:TPU:8, one launch (start us, length us, event | category | flops | bytes accessed | tf_op | source)
XLA Modules:
  0.0 785.8 jit_solution(10798245600985077650)
XLA Ops:
  6.5 5.9 convolution_convert_fusion.1
  12.5 1.7 reshape.173
  14.2 1.0 fusion.55
  15.3 0.7 broadcast_compare_fusion
  16.4 163.7 %gather_fusion.1 = bf16[16384]{0:T(1024)(128)(2,1)S(1)} fusion(bf16[32,8,4,128]{3,1,0,2:T(8,128)(2,1)S(1)} %get-tuple-element.34, s32[16384]{0:T(1024)S(1)} %bitcast.146), kind=kCustom, calls=%fused_computation.2.clone | custom fusion | bytes 327680 | tf_op jit(solution)/shard_map/jit(take_along_axis)/gather | solution.py:34
  180.1 163.7 %gather_fusion.2 = bf16[16384]{0:T(1024)(128)(2,1)S(1)} fusion(bf16[32,8,4,128]{3,1,0,2:T(8,128)(2,1)S(1)} %get-tuple-element.20, s32[16384]{0:T(1024)S(1)} %bitcast.147), kind=kCustom, calls=%fused_computation.3.clone | custom fusion | bytes 327680 | tf_op jit(solution)/shard_map/jit(take_along_axis)/gather | solution.py:34
  344.6 4.1 collective-permute-start
  348.6 4.0 collective-permute-start.1
  352.9 3.2 collective-permute-start.3
  356.1 2.6 collective-permute-start.4
  358.7 0.7 select_bitcast_fusion.1
  359.6 22.2 %gather_fusion.5 = bf16[2048]{0:T(1024)(128)(2,1)S(1)} fusion(bf16[4,64,4,128]{3,1,0,2:T(8,128)(2,1)S(1)} %bitcast.155, s32[2048]{0:T(1024)S(1)} %bitcast.151), kind=kCustom, calls=%fused_computation.5.clone | custom fusion | bytes 40960 | tf_op jit(solution)/shard_map/jit(take_along_axis)/gather | solution.py:34
  381.7 22.2 %gather_fusion.4 = bf16[2048]{0:T(1024)(128)(2,1)S(1)} fusion(bf16[4,64,4,128]{3,1,0,2:T(8,128)(2,1)S(1)} %bitcast.154, s32[2048]{0:T(1024)S(1)} %bitcast.152), kind=kCustom, calls=%fused_computation.4.clone | custom fusion | bytes 40960 | tf_op jit(solution)/shard_map/jit(take_along_axis)/gather | solution.py:34
  403.9 22.2 %gather_fusion.3 = bf16[2048]{0:T(1024)(128)(2,1)S(1)} fusion(bf16[4,64,4,128]{3,1,0,2:T(8,128)(2,1)S(1)} %bitcast.149, s32[2048]{0:T(1024)S(1)} %bitcast.153), kind=kCustom, calls=%fused_computation.1.clone | custom fusion | bytes 40960 | tf_op jit(solution)/shard_map/jit(take_along_axis)/gather | solution.py:34
  426.2 0.9 stack.8
  427.1 7.5 all-to-all-start
  434.9 1.3 fusion.59
  436.2 0.6 iota_compare_fusion.1
  436.9 0.6 iota_compare_fusion
  437.7 1.8 copy.69
  439.5 236.0 %gather_fusion = bf16[16384]{0:T(1024)(128)(2,1)} fusion(bf16[32,8,4,128]{3,1,0,2:T(8,128)(2,1)S(1)} %bitcast.150, s32[16384]{0:T(1024)S(1)} %bitcast.148), kind=kCustom, calls=%fused_computation.clone | custom fusion | bytes 327680 | tf_op jit(solution)/shard_map/jit(take_along_axis)/gather | solution.py:34
  675.6 0.7 broadcast_in_dim.167
  676.4 0.7 broadcast_in_dim.173
  677.1 1.5 collective-permute-start.5
  678.6 0.8 constant_dynamic-update-slice_fusion.14
  679.5 0.9 constant_dynamic-update-slice_fusion.13
  680.4 3.9 collective-permute-start.7
  684.3 0.9 constant_dynamic-update-slice_fusion.12
  685.8 0.9 constant_dynamic-update-slice_fusion.11
  686.8 0.9 constant_dynamic-update-slice_fusion.10
  687.6 3.4 collective-permute-start.10
  691.0 1.5 collective-permute-start.11
  692.6 4.2 collective-permute-start.12
  696.8 3.7 collective-permute-start.13
  701.0 5.7 collective-permute-done.13
  706.7 0.9 copy-done.5
  707.7 1.1 fusion.58
  709.3 1.2 convolution_bitcast_fusion.1
  710.5 0.8 broadcast_bitcast_fusion
  711.3 2.0 copy.63
  713.4 1.2 fusion.56
  715.7 0.9 broadcast_in_dim.183
  716.6 2.0 copy.65
  718.6 1.6 fusion.4
  720.3 1.7 convolution_convert_fusion
  722.0 52.4 %all-reduce.2.cloned.1.call-done = bf16[256,2048]{1,0:T(8,128)(2,1)} async-done(((bf16[256,2048]{1,0:T(8,128)(2,1)}), bf16[256,2048]{1,0:T(8,128)(2,1)}) %all-reduce.2.cloned.1.call-update) | async-done | bytes 1048592 | tf_op jit(solution)/shard_map/psum | solution.py:97
  774.4 2.0 multiply_reduce_fusion
  776.4 2.5 convolution_divide_fusion
  (93 shorter events, 5.2 us)
Async XLA Ops:
  6.5 713.8 %copy-start = (bf16[512,2048]{1,0:T(8,128)(2,1)S(1)}, bf16[512,2048]{1,0:T(8,128)(2,1)}, u32[]{:S(2)}) copy-start(bf16[512,2048]{1,0:T(8,128)(2,1)} %param.13) | copy-start | bytes 6291460
  6.5 8.7 %copy-start.6 = (s32[4]{0:T(128)S(1)}, s32[4]{0:T(128)}, u32[]{:S(2)}) copy-start(s32[4]{0:T(128)} %param.16) | copy-start | bytes 52
  6.5 8.7 %copy-start.9 = (s32[4]{0:T(128)S(1)}, s32[4]{0:T(128)}, u32[]{:S(2)}) copy-start(s32[4]{0:T(128)} %param.17) | copy-start | bytes 52
  15.2 0.9 copy-start.1
  15.2 1.1 copy-start.3
  15.2 328.6 %copy-start.8 = (s32[4]{0:T(128)}, s32[4]{0:T(128)S(1)}, u32[]{:S(2)}) copy-start(s32[4]{0:T(128)S(1)} %broadcast_add_fusion.1) | copy-start | bytes 52
  15.9 327.9 %copy-start.7 = (pred[4]{0:T(512)(128)(4,1)}, pred[4]{0:T(512)(128)(4,1)S(1)}, u32[]{:S(2)}) copy-start(pred[4]{0:T(512)(128)(4,1)S(1)} %get-tuple-element.36) | copy-start | bytes 16
  180.1 178.6 %copy-start.2 = (bf16[256,1,4,128]{3,2,0,1:T(4,128)(2,1)S(1)}, bf16[256,1,4,128]{3,2,0,1:T(4,128)(2,1)}, u32[]{:S(2)}) copy-start(bf16[256,1,4,128]{3,2,0,1:T(4,128)(2,1)} %get-tuple-element.12) | copy-start | bytes 786436
  344.6 332.6 %collective-permute-start = (bf16[2,32,4,128]{3,1,2,0:T(8,128)(2,1)}, bf16[2,32,4,128]{3,1,2,0:T(8,128)(2,1)}, u32[]{:S(2)}, u32[]{:S(2)}) collective-permute-start(bf16[2,32,4,128]{3,1,2,0:T(8,128)(2,1)} %pad_maximum_fusion), channel_id=1, source_target_pairs={{228,0},{232,4},{236,8},{240,12},{244,16},{248,20},{252,24},{0,28}... | collective-permute-start | bytes 196616 | tf_op jit(solution)/shard_map/ppermute | solution.py:12
  348.6 330.8 %collective-permute-start.1 = (bf16[2,32,4,128]{3,1,2,0:T(8,128)(2,1)}, bf16[2,32,4,128]{3,1,2,0:T(8,128)(2,1)}, u32[]{:S(2)}, u32[]{:S(2)}) collective-permute-start(bf16[2,32,4,128]{3,1,2,0:T(8,128)(2,1)} %pad_maximum_fusion), channel_id=1, source_target_pairs={{232,0},{236,4},{240,8},{244,12},{248,16},{252,20},{0,24},{4,28},{... | collective-permute-start | bytes 196616 | tf_op jit(solution)/shard_map/ppermute | solution.py:12
  352.7 327.7 %collective-permute-start.2 = (bf16[2,32,4,128]{3,1,2,0:T(8,128)(2,1)}, bf16[2,32,4,128]{3,1,2,0:T(8,128)(2,1)}, u32[]{:S(2)}, u32[]{:S(2)}) collective-permute-start(bf16[2,32,4,128]{3,1,2,0:T(8,128)(2,1)} %pad_maximum_fusion), channel_id=1, source_target_pairs={{236,0},{240,4},{244,8},{248,12},{252,16},{0,20},{4,24},{8,28},{12... | collective-permute-start | bytes 196616 | tf_op jit(solution)/shard_map/ppermute | solution.py:12
  352.9 332.2 %collective-permute-start.3 = (bf16[2,32,4,128]{3,1,2,0:T(8,128)(2,1)}, bf16[2,32,4,128]{3,1,2,0:T(8,128)(2,1)}, u32[]{:S(2)}, u32[]{:S(2)}) collective-permute-start(bf16[2,32,4,128]{3,1,2,0:T(8,128)(2,1)} %pad_maximum_fusion), channel_id=1, source_target_pairs={{240,0},{244,4},{248,8},{252,12},{0,16},{4,20},{8,24},{12,28},{16,... | collective-permute-start | bytes 196616 | tf_op jit(solution)/shard_map/ppermute | solution.py:12
  356.1 330.5 %collective-permute-start.4 = (bf16[2,32,4,128]{3,1,2,0:T(8,128)(2,1)}, bf16[2,32,4,128]{3,1,2,0:T(8,128)(2,1)}, u32[]{:S(2)}, u32[]{:S(2)}) collective-permute-start(bf16[2,32,4,128]{3,1,2,0:T(8,128)(2,1)} %pad_maximum_fusion), channel_id=1, source_target_pairs={{244,0},{248,4},{252,8},{0,12},{4,16},{8,20},{12,24},{16,28},{20,3... | collective-permute-start | bytes 196616 | tf_op jit(solution)/shard_map/ppermute | solution.py:12
  381.7 44.3 %copy-start.10 = (pred[4]{0:T(512)(128)(4,1)S(1)}, pred[4]{0:T(512)(128)(4,1)}, u32[]{:S(2)}) copy-start(pred[4]{0:T(512)(128)(4,1)} %get-tuple-element.35) | copy-start | bytes 16
  427.1 286.2 %all-to-all-start = ((bf16[64,2,4,4,128]{4,2,3,1,0:T(4,128)(2,1)}), bf16[64,2,4,4,128]{4,2,3,1,0:T(4,128)(2,1)}, u32[]{:S(2)}, u32[]{:S(2)}) async-start(bf16[64,2,4,4,128]{4,2,3,1,0:T(4,128)(2,1)} %stack.8), calls=%async_computation | async-start | bytes 1048576 | tf_op jit(solution)/shard_map/all_to_all | solution.py:82
  434.7 339.7 %all-reduce.2.cloned.1.call-start = ((), (), s32[]{:S(2)}) async-start(), calls=%async_computation.1 | async-start | bytes 2097152 | tf_op jit(solution)/shard_map/psum | solution.py:97
  677.1 10.5 %collective-permute-start.5 = (bf16[2,32,4,128]{3,1,2,0:T(8,128)(2,1)}, bf16[2,32,4,128]{3,1,2,0:T(8,128)(2,1)S(1)}, u32[]{:S(2)}, u32[]{:S(2)}) collective-permute-start(bf16[2,32,4,128]{3,1,2,0:T(8,128)(2,1)} %pad_maximum_fusion), channel_id=1, source_target_pairs={{248,0},{252,4},{0,8},{4,12},{8,16},{12,20},{16,24},{20,28},{24,32... | collective-permute-start | bytes 196616 | tf_op jit(solution)/shard_map/ppermute | solution.py:12
  679.4 11.6 %collective-permute-start.6 = (bf16[2,32,4,128]{3,1,2,0:T(8,128)(2,1)}, bf16[2,32,4,128]{3,1,2,0:T(8,128)(2,1)S(1)}, u32[]{:S(2)}, u32[]{:S(2)}) collective-permute-start(bf16[2,32,4,128]{3,1,2,0:T(8,128)(2,1)} %pad_maximum_fusion), channel_id=1, source_target_pairs={{252,0},{0,4},{4,8},{8,12},{12,16},{16,20},{20,24},{24,28},{28,32}... | collective-permute-start | bytes 196616 | tf_op jit(solution)/shard_map/ppermute | solution.py:12
  680.4 12.2 %collective-permute-start.7 = (bf16[2,32,4,128]{3,1,2,0:T(8,128)(2,1)}, bf16[2,32,4,128]{3,1,2,0:T(8,128)(2,1)S(1)}, u32[]{:S(2)}, u32[]{:S(2)}) collective-permute-start(bf16[2,32,4,128]{3,1,2,0:T(8,128)(2,1)} %pad_maximum_fusion), channel_id=1, source_target_pairs={{4,0},{8,4},{12,8},{16,12},{20,16},{24,20},{28,24},{32,28},{36,32}... | collective-permute-start | bytes 196616 | tf_op jit(solution)/shard_map/ppermute | solution.py:12
  685.2 11.7 %collective-permute-start.8 = (bf16[2,32,4,128]{3,1,2,0:T(8,128)(2,1)}, bf16[2,32,4,128]{3,1,2,0:T(8,128)(2,1)S(1)}, u32[]{:S(2)}, u32[]{:S(2)}) collective-permute-start(bf16[2,32,4,128]{3,1,2,0:T(8,128)(2,1)} %pad_maximum_fusion), channel_id=1, source_target_pairs={{8,0},{12,4},{16,8},{20,12},{24,16},{28,20},{32,24},{36,28},{40,32... | collective-permute-start | bytes 196616 | tf_op jit(solution)/shard_map/ppermute | solution.py:12
  686.7 13.9 %collective-permute-start.9 = (bf16[2,32,4,128]{3,1,2,0:T(8,128)(2,1)}, bf16[2,32,4,128]{3,1,2,0:T(8,128)(2,1)S(1)}, u32[]{:S(2)}, u32[]{:S(2)}) collective-permute-start(bf16[2,32,4,128]{3,1,2,0:T(8,128)(2,1)} %pad_maximum_fusion), channel_id=1, source_target_pairs={{12,0},{16,4},{20,8},{24,12},{28,16},{32,20},{36,24},{40,28},{44,3... | collective-permute-start | bytes 196616 | tf_op jit(solution)/shard_map/ppermute | solution.py:12
  687.6 12.9 %collective-permute-start.10 = (bf16[2,32,4,128]{3,1,2,0:T(8,128)(2,1)}, bf16[2,32,4,128]{3,1,2,0:T(8,128)(2,1)S(1)}, u32[]{:S(2)}, u32[]{:S(2)}) collective-permute-start(bf16[2,32,4,128]{3,1,2,0:T(8,128)(2,1)} %pad_maximum_fusion), channel_id=1, source_target_pairs={{16,0},{20,4},{24,8},{28,12},{32,16},{36,20},{40,24},{44,28},{48,3... | collective-permute-start | bytes 196616 | tf_op jit(solution)/shard_map/ppermute | solution.py:12
  691.0 9.6 %collective-permute-start.11 = (bf16[2,32,4,128]{3,1,2,0:T(8,128)(2,1)}, bf16[2,32,4,128]{3,1,2,0:T(8,128)(2,1)S(1)}, u32[]{:S(2)}, u32[]{:S(2)}) collective-permute-start(bf16[2,32,4,128]{3,1,2,0:T(8,128)(2,1)} %pad_maximum_fusion), channel_id=1, source_target_pairs={{20,0},{24,4},{28,8},{32,12},{36,16},{40,20},{44,24},{48,28},{52,3... | collective-permute-start | bytes 196616 | tf_op jit(solution)/shard_map/ppermute | solution.py:12
  692.6 8.4 %collective-permute-start.12 = (bf16[2,32,4,128]{3,1,2,0:T(8,128)(2,1)}, bf16[2,32,4,128]{3,1,2,0:T(8,128)(2,1)S(1)}, u32[]{:S(2)}, u32[]{:S(2)}) collective-permute-start(bf16[2,32,4,128]{3,1,2,0:T(8,128)(2,1)} %pad_maximum_fusion), channel_id=1, source_target_pairs={{24,0},{28,4},{32,8},{36,12},{40,16},{44,20},{48,24},{52,28},{56,3... | collective-permute-start | bytes 196616 | tf_op jit(solution)/shard_map/ppermute | solution.py:12
  696.8 9.8 %collective-permute-start.13 = (bf16[2,32,4,128]{3,1,2,0:T(8,128)(2,1)}, bf16[2,32,4,128]{3,1,2,0:T(8,128)(2,1)S(1)}, u32[]{:S(2)}, u32[]{:S(2)}) collective-permute-start(bf16[2,32,4,128]{3,1,2,0:T(8,128)(2,1)} %pad_maximum_fusion), channel_id=1, source_target_pairs={{28,0},{32,4},{36,8},{40,12},{44,16},{48,20},{52,24},{56,28},{60,3... | collective-permute-start | bytes 196616 | tf_op jit(solution)/shard_map/ppermute | solution.py:12
  706.7 0.9 copy-start.5
  715.4 61.0 %copy-start.11 = (f32[2048]{0:T(1024)S(1)}, f32[2048]{0:T(1024)}, u32[]{:S(2)}) copy-start(f32[2048]{0:T(1024)} %param.14) | copy-start | bytes 24580
  720.3 56.1 %copy-start.4 = (bf16[256,2048]{1,0:T(8,128)(2,1)S(1)}, bf16[256,2048]{1,0:T(8,128)(2,1)}, u32[]{:S(2)}) copy-start(bf16[256,2048]{1,0:T(8,128)(2,1)} %param.11) | copy-start | bytes 3145732
Sparse Core Ops, SparseCore 0:
  722.2 52.1 all-reduce.1
